TPU v7x, 32 devices: a whole 2x2x4 slice. The times are simulated.
32 devices in a mesh: rows: 8 (over y, x, core), cols: 4 (over z).
Axes of the slice: x: 2, y: 2, z: 4, core: 2. Of those that a mesh axis runs over, the one named last changes fastest.
Arguments:
- block_values: bfloat16 [16384, 128], P(('rows', 'cols')), may hold values from -6 to 6
- block_length: int32 [16384], P(('rows', 'cols')), may hold values from 1 to 128
- block_owner: int32 [16384], P(('rows', 'cols')), may hold values from 0 to 4095, as said below
- block_second: int32 [16384], P(('rows', 'cols')), may hold values from 0 to 4095, as said below
- block_third: int32 [16384, 128], P(('rows', 'cols')), may hold values from 0 to 8191
- live_blocks: int32 [32], P(('rows', 'cols')), may hold values from 1 to 512, as said below
- second_factor: bfloat16 [4096, 256], P('cols', 'rows')
- third_factor: bfloat16 [8192, 256], P('cols', 'rows'), may hold values from -6 to 6
Outputs:
- first_factor: float32 [4096, 256], P('cols', 'rows')
Inputs may be any that keep to these rules, and one draw needn't show every extreme that they name: `block_owner`: slot b lies on device d = b // 512 with index r along rows; its row lies in r * 4096 // 8 up to (r + 1) * 4096 // 8 - 1, the device's mode-1 slab. `block_second`: slot b lies on device d = b // 512 with index c along cols; its row lies in c * 4096 // 4 up to (c + 1) * 4096 // 4 - 1. `live_blocks`: some device uses all 512 slots in every draw.
All inputs are finite; a program needn't handle non-finite values.
Results may differ from a plain program's by a relative error of at most 0.0003.
Values may be sent and summed in bfloat16 or wider, within the bound.
A program may use at most 128 MiB of HBM per device.

v0:
```python
import jax
import jax.numpy as jnp
from jax import lax
from jax.sharding import PartitionSpec as P

I_DEV = 128


def gram_product(left, right):
    contract = (((0,), (0,)), ((), ()))
    return lax.dot_general(left, right, contract, preferred_element_type=jnp.float32)


def block_fold(values, third, table):
    group = values.shape[0]
    width = values.shape[1]
    picked = table[third.reshape(group * width)]
    scaled = values.reshape(group * width, 1).astype(jnp.float32) * picked.astype(jnp.float32)
    return jnp.sum(scaled.reshape(group, width, picked.shape[1]), axis=1)


def per_device(
    block_values,
    block_length,
    block_owner,
    block_second,
    block_third,
    live_blocks,
    second_factor,
    third_factor,
):
    n_rows = lax.axis_size("rows")
    n_cols = lax.axis_size("cols")
    row_at = lax.axis_index("rows")
    col_at = lax.axis_index("cols")
    contract = (((0,), (0,)), ((), ()))
    width = block_values.shape[1]
    lane = jnp.arange(width, dtype=jnp.int32)
    slab = I_DEV * n_cols
    owned = jnp.arange(slab, dtype=jnp.int32)
    second_range = lax.all_gather(second_factor, "rows", axis=1, tiled=True)
    third_part = lax.all_gather(third_factor, "cols", axis=0, tiled=True)
    third_whole = lax.all_gather(third_part, "rows", axis=1, tiled=True)
    range_rows = second_range.shape[0]
    local_gram = gram_product(second_range, second_range)
    gram_second = lax.psum(local_gram, "cols") / (range_rows * n_cols)
    gram_third = gram_product(third_whole, third_whole) / third_whole.shape[0]
    gram = gram_second * gram_third
    nblk = block_values.shape[0]
    group = min(nblk, 128)
    count = live_blocks[0]

    def accumulate(step, total):
        start = step * group
        values = lax.dynamic_slice_in_dim(block_values, start, group, 0)
        lengths = lax.dynamic_slice_in_dim(block_length, start, group, 0)
        third = lax.dynamic_slice_in_dim(block_third, start, group, 0)
        second = lax.dynamic_slice_in_dim(block_second, start, group, 0)
        owner = lax.dynamic_slice_in_dim(block_owner, start, group, 0)
        slot = start + jnp.arange(group, dtype=jnp.int32)
        live = (lane[None, :] < lengths[:, None]) & (slot < count)[:, None]
        values = jnp.where(live, values, jnp.zeros((), jnp.bfloat16))
        fold = block_fold(values, third, third_whole)
        contrib = second_range[second - col_at * range_rows].astype(jnp.float32) * fold
        onehot = ((owner - row_at * slab)[:, None] == owned[None, :]).astype(jnp.float32)
        return total + lax.dot_general(
            onehot,
            contrib,
            contract,
            precision=lax.Precision.HIGHEST,
            preferred_element_type=jnp.float32,
        )

    start_total = jnp.zeros((slab, gram.shape[0]), jnp.float32)
    partial_rows = lax.fori_loop(0, (count + group - 1) // group, accumulate, start_total)
    mine = lax.psum_scatter(partial_rows, "cols", scatter_dimension=0, tiled=True)
    factor = jnp.linalg.cholesky(gram)
    solved = jax.scipy.linalg.cho_solve((factor, True), mine.T).T
    moved = lax.all_to_all(
        lax.all_to_all(solved, "rows", split_axis=1, concat_axis=0, tiled=True),
        "cols",
        split_axis=0,
        concat_axis=0,
        tiled=True,
    )
    share = n_rows // n_cols
    owned_rows = mine.shape[0]
    reordered = moved.reshape(n_cols, share, owned_rows, moved.shape[1]).transpose(1, 0, 2, 3)
    return reordered.reshape(n_rows * owned_rows, moved.shape[1])


def solution(mesh):
    return jax.shard_map(
        per_device,
        mesh=mesh,
        in_specs=(
            P(("rows", "cols"), None),
            P(("rows", "cols")),
            P(("rows", "cols")),
            P(("rows", "cols")),
            P(("rows", "cols"), None),
            P(("rows", "cols")),
            P("cols", "rows"),
            P("cols", "rows"),
        ),
        out_specs=P("cols", "rows"),
        check_vma=False,
    )
```

profile of v0, /device:TPU:0, one launch (start us, length us, event | category | flops | bytes accessed | tf_op | source)
XLA Modules:
  0.0 476.4 jit_solution(10479192141841204088)
XLA Ops:
  7.4 11.6 %all_gather.9 = bf16[1024,256]{0,1:T(8,128)(2,1)S(1)} all-gather(bf16[1024,32]{0,1:T(8,128)(2,1)} %param.16), channel_id=1, replica_groups=mesh['rows'=8,'cols'=4] {'rows'}, dimensions={1}, use_global_device_ids=true | all-gather | bytes 589824 | tf_op jit(solution)/shard_map/all_gather | solution.py:41
  19.0 1.1 fusion.24
  20.1 20.9 %all_gather.10 = bf16[8192,32]{0,1:T(8,128)(2,1)} all-gather(bf16[2048,32]{0,1:T(8,128)(2,1)} %param.17), channel_id=1, replica_groups=mesh['rows'=8,'cols'=4] {'cols'}, dimensions={0}, use_global_device_ids=true | all-gather | bytes 655360 | tf_op jit(solution)/shard_map/all_gather | solution.py:42
  42.0 15.7 %all-reduce.3.cloned.1.call-done = f32[256,256]{0,1:T(8,128)} async-done(((f32[256,256]{0,1:T(8,128)}), f32[256,256]{0,1:T(8,128)}) %all-reduce.3.cloned.1.call-update) | async-done | bytes 262160 | tf_op jit(solution)/shard_map/psum | solution.py:46
  57.7 18.4 %all-gather.2.cloned.1.call-done = bf16[8192,256]{0,1:T(8,128)(2,1)} async-done(((bf16[8192,32]{0,1:T(8,128)(2,1)}), bf16[8192,256]{0,1:T(8,128)(2,1)}) %all-gather.2.cloned.1.call-update) | async-done | bytes 4194320 | tf_op jit(solution)/shard_map/all_gather | solution.py:43
  76.1 4.7 fusion.11
  81.1 11.7 %cholesky.50 = f32[128,128]{1,0:T(8,128)S(1)} custom-call(f32[128,128]{1,0:T(8,128)S(1)} %cholesky.118), custom_call_target="Cholesky" | custom-call | tf_op jit(solution)/shard_map/jit(cholesky)/cholesky | solution.py:77
  92.8 9.8 %custom-call.18 = f32[1,128,128]{1,2,0:T(8,128)S(1)} custom-call(f32[1,128,128]{2,1,0:T(8,128)S(1)} %get-tuple-element.274), custom_call_target="InvertDiagBlocksLowerTriangular" | custom-call | tf_op jit(solution)/shard_map/jit(cholesky)/cholesky | solution.py:77
  103.1 11.7 %cholesky.105 = f32[128,128]{1,0:T(8,128)S(1)} custom-call(f32[128,128]{1,0:T(8,128)S(1)} %convolution_subtract_fusion.2), custom_call_target="Cholesky" | custom-call | tf_op jit(solution)/shard_map/jit(cholesky)/cholesky | solution.py:77
  114.8 6.4 %copy.34 = bf16[8192,256]{1,0:T(8,128)(2,1)} copy(bf16[8192,256]{0,1:T(8,128)(2,1)} %all-gather.2.cloned.1.call-done) | data formatting | bytes 8388608
  121.3 223.8 %while.15 = (s32[]{:T(128)}, f32[512,256]{1,0:T(8,128)S(1)}, s32[]{:T(128)}, s32[512]{0:T(512)}, s32[]{:T(128)}, /*index=5*/s32[512]{0:T(512)}, s32[]{:T(128)}, ...) while((s32[]{:T(128)}, f32[512,256]{1,0:T(8,128)S(1)}, ...), condition=%wide.region_7.8_spmd.clone, body=%wide.region_5.7_spmd.clone.sunk | while | flops 214271872 | bytes 27305452 | solution.py:75
  122.9 0.9 fusion.42
  124.7 63.5 %gather_fusion = bf16[16384,256]{1,0:T(8,128)(2,1)} fusion(bf16[8192,256]{1,0:T(8,128)(2,1)} %get-tuple-element.438, s32[16384]{0:T(1024)S(1)} %broadcast_clamp_fusion.2), kind=kCustom, calls=%fused_computation.1.clone.clone.1 | custom fusion | bytes 16842752 | tf_op jit(solution)/shard_map/while/body/gather | solution.py:17
  188.2 5.5 %fusion.43 = f32[128,256]{1,0:T(8,128)S(1)} fusion(f32[128,128]{1,0:T(8,128)S(1)} %fusion.42, bf16[16384,256]{1,0:T(8,128)(2,1)} %gather_fusion), kind=kLoop, calls=%fused_computation.7.clone.1 | loop fusion | flops 12550144 | bytes 8585216 | tf_op jit(solution)/shard_map/while/body/reduce_sum | solution.py:19
  197.4 0.9 fusion.42
  198.3 0.9 constant_dynamic-slice_fusion.5
  199.2 63.5 %gather_fusion = bf16[16384,256]{1,0:T(8,128)(2,1)} fusion(bf16[8192,256]{1,0:T(8,128)(2,1)} %get-tuple-element.438, s32[16384]{0:T(1024)S(1)} %broadcast_clamp_fusion.2), kind=kCustom, calls=%fused_computation.1.clone.clone.1 | custom fusion | bytes 16842752 | tf_op jit(solution)/shard_map/while/body/gather | solution.py:17
  262.8 5.5 %fusion.43 = f32[128,256]{1,0:T(8,128)S(1)} fusion(f32[128,128]{1,0:T(8,128)S(1)} %fusion.42, bf16[16384,256]{1,0:T(8,128)(2,1)} %gather_fusion), kind=kLoop, calls=%fused_computation.7.clone.1 | loop fusion | flops 12550144 | bytes 8585216 | tf_op jit(solution)/shard_map/while/body/reduce_sum | solution.py:19
  271.9 0.9 fusion.42
  272.8 0.9 constant_dynamic-slice_fusion.5
  273.8 63.5 %gather_fusion = bf16[16384,256]{1,0:T(8,128)(2,1)} fusion(bf16[8192,256]{1,0:T(8,128)(2,1)} %get-tuple-element.438, s32[16384]{0:T(1024)S(1)} %broadcast_clamp_fusion.2), kind=kCustom, calls=%fused_computation.1.clone.clone.1 | custom fusion | bytes 16842752 | tf_op jit(solution)/shard_map/while/body/gather | solution.py:17
  337.3 5.5 %fusion.43 = f32[128,256]{1,0:T(8,128)S(1)} fusion(f32[128,128]{1,0:T(8,128)S(1)} %fusion.42, bf16[16384,256]{1,0:T(8,128)(2,1)} %gather_fusion), kind=kLoop, calls=%fused_computation.7.clone.1 | loop fusion | flops 12550144 | bytes 8585216 | tf_op jit(solution)/shard_map/while/body/reduce_sum | solution.py:19
  345.1 1.0 copy.35
  348.2 3.9 while.14
  348.8 1.3 bitcast_dynamic-update-slice_fusion.2
  350.7 1.3 bitcast_dynamic-update-slice_fusion.2
  352.1 19.7 %custom-call.19 = f32[2,128,128]{1,2,0:T(8,128)S(1)} custom-call(f32[2,128,128]{2,1,0:T(8,128)S(1)} %get-tuple-element.189), custom_call_target="InvertDiagBlocksLowerTriangular" | custom-call | tf_op jit(solution)/shard_map/jit(_cho_solve)/triangular_solve | solution.py:78
  371.8 70.9 %reduce-scatter.2.cloned.1.call-done = f32[128,256]{0,1:T(8,128)} async-done(((f32[512,256]{0,1:T(8,128)}), f32[128,256]{0,1:T(8,128)}) %reduce-scatter.2.cloned.1.call-update) | async-done | bytes 131088 | tf_op jit(solution)/shard_map/reduce_scatter | solution.py:76
  442.6 1.1 fusion.13
  443.7 1.0 convolution_subtract_fusion.1
  445.8 11.8 %all_to_all.25 = f32[128,8,32]{0,2,1:T(8,128)S(1)} all-to-all(f32[128,8,32]{0,2,1:T(8,128)S(1)} %bitcast.67), channel_id=1, replica_groups=mesh['rows'=8,'cols'=4] {'rows'}, dimensions={1} | all-to-all | bytes 262144 | tf_op jit(solution)/shard_map/all_to_all | solution.py:80
  457.8 10.3 %all_to_all.26 = f32[4,256,32]{1,2,0:T(8,128)S(1)} all-to-all(f32[4,256,32]{1,2,0:T(8,128)S(1)} %copy.37), channel_id=1, replica_groups=mesh['rows'=8,'cols'=4] {'cols'}, dimensions={0} | all-to-all | bytes 262144 | tf_op jit(solution)/shard_map/all_to_all | solution.py:79
  (61 shorter events, 17.3 us)
Async XLA Ops:
  7.4 50.3 %all-reduce.3.cloned.1.call-start = ((), (), s32[]{:S(2)}) async-start(), calls=%async_computation.3 | async-start | bytes 524288 | tf_op jit(solution)/shard_map/psum | solution.py:46
  20.1 56.0 %all-gather.2.cloned.1.call-start = ((), (), s32[]{:S(2)}) async-start(), calls=%async_computation.4 | async-start | bytes 4718592 | tf_op jit(solution)/shard_map/all_gather | solution.py:43
  41.0 401.6 %reduce-scatter.2.cloned.1.call-start = ((), (), s32[]{:S(2)}) async-start(), calls=%async_computation.5 | async-start | bytes 655360 | tf_op jit(solution)/shard_map/reduce_scatter | solution.py:76
Sparse Core Ops, SparseCore 0:
  20.2 37.4 all-reduce.2
  346.2 96.3 reduce-scatter.1
Sparse Core Ops, SparseCore 1:
  41.1 34.9 all-gather.1
where the time goes:
time: 478 us; the launch traced here: 476 us
  local copies, waits for them, and re-layouts  211 us (44%)
  waiting for transfers between devices  105 us (22%)
  other arithmetic  77.3 us (16%)
  blocking collectives  54.6 us (11%)
  between operations  17 us (4%)
  matrix products  11.3 us (2%)
    gather x3, local copies, waits for them, and re-layouts, block_fold(): picked = table[third.reshape(group * width)]  191 us
    reduce_scatter x1, waiting for transfers between devices, per_device(): lax.psum_scatter(partial_rows, 'cols', scatter_dimension=0, tiled=True)  70.9 us
    another operation x6, other arithmetic, per_device(): factor = jnp.linalg.cholesky(gram)  34 us
    all_gather x1, blocking collectives, per_device(): third_part = lax.all_gather(third_factor, 'cols', axis=0, tiled=True)  20.9 us
    another operation x4, other arithmetic, per_device(): solved = jax.scipy.linalg.cho_solve((factor, True), mine.T).T  19.7 us
    all_gather x1, waiting for transfers between devices, per_device(): third_whole = lax.all_gather(third_part, 'rows', axis=1, tiled=True)  18.4 us
    reduce_sum x3, other arithmetic, block_fold(): return jnp.sum(scaled.reshape(group, width, picked.shape[1]), axis=1)  16.4 us
    psum x1, waiting for transfers between devices, per_device(): gram_second = lax.psum(local_gram, 'cols') / (range_rows * n_cols)  15.7 us
  transfers between devices with their start and end apart: 3, of which 3 were waited for; matrix products, arithmetic and copies ran while one was open for 5% of the time, Pallas kernels for 0%

commit v1 on v0

--- a/solution.py
+++ b/solution.py
@@ -40,7 +40,9 @@
     owned = jnp.arange(slab, dtype=jnp.int32)
     second_range = lax.all_gather(second_factor, "rows", axis=1, tiled=True)
     third_part = lax.all_gather(third_factor, "cols", axis=0, tiled=True)
-    third_whole = lax.all_gather(third_part, "rows", axis=1, tiled=True)
+    third_whole = jnp.concatenate(
+        lax.all_to_all(jnp.stack([third_part] * lax.axis_size("rows")), "rows", 0, 0), axis=1
+    )
     range_rows = second_range.shape[0]
     local_gram = gram_product(second_range, second_range)
     gram_second = lax.psum(local_gram, "cols") / (range_rows * n_cols)

time: 478 us -> 517 us (1.082)
  blocking collectives: 54.6 us -> 92.9 us
    all_gather x1, blocking collectives: 11.6 us -> 53.3 us  [per_device(): second_range = lax.all_gather(second_factor, 'rows', axis=1, tiled=True)]
    all_gather x1 -> x0, waiting for transfers between devices: 18.4 us -> none  [per_device(): third_whole = lax.all_gather(third_part, 'rows', axis=1, tiled=True)]
    psum x1, waiting for transfers between devices: 15.7 us -> 29.2 us  [per_device(): gram_second = lax.psum(local_gram, 'cols') / (range_rows * n_cols)]
  transfers between devices with their start and end apart: 3 -> 3, of which waited for: 3 -> 2; matrix products, arithmetic and copies ran while one was open for 5% -> 6% of each run, Pallas kernels for 0% -> 0%
where the time goes in v1:
time: 517 us; the launch traced here: 515 us
  local copies, waits for them, and re-layouts  213 us (41%)
  waiting for transfers between devices  100 us (19%)
  blocking collectives  92.9 us (18%)
  other arithmetic  77.4 us (15%)
  between operations  15.6 us (3%)
  matrix products  11.3 us (2%)
    gather x3, local copies, waits for them, and re-layouts, block_fold(): picked = table[third.reshape(group * width)]  190 us
    reduce_scatter x1, waiting for transfers between devices, per_device(): lax.psum_scatter(partial_rows, 'cols', scatter_dimension=0, tiled=True)  70.7 us
    all_gather x1, blocking collectives, per_device(): second_range = lax.all_gather(second_factor, 'rows', axis=1, tiled=True)  53.3 us
    another operation x6, other arithmetic, per_device(): factor = jnp.linalg.cholesky(gram)  34 us
    psum x1, waiting for transfers between devices, per_device(): gram_second = lax.psum(local_gram, 'cols') / (range_rows * n_cols)  29.2 us
    another operation x4, other arithmetic, per_device(): solved = jax.scipy.linalg.cho_solve((factor, True), mine.T).T  19.7 us
    all_gather x1, blocking collectives, per_device(): third_part = lax.all_gather(third_factor, 'cols', axis=0, tiled=True)  17.6 us
    reduce_sum x3, other arithmetic, block_fold(): return jnp.sum(scaled.reshape(group, width, picked.shape[1]), axis=1)  16.5 us
  transfers between devices with their start and end apart: 3, of which 2 were waited for; matrix products, arithmetic and copies ran while one was open for 6% of the time, Pallas kernels for 0%

profile of v1, /device:TPU:0, one launch (start us, length us, event | category | flops | bytes accessed | tf_op | source)
XLA Modules:
  0.0 515.3 jit_solution(12662290807586055291)
XLA Ops:
  6.5 17.6 %all_gather.7 = bf16[8192,32]{0,1:T(8,128)(2,1)S(1)} all-gather(bf16[2048,32]{0,1:T(8,128)(2,1)} %param.17), channel_id=1, replica_groups=mesh['rows'=8,'cols'=4] {'cols'}, dimensions={0}, use_global_device_ids=true | all-gather | bytes 655360 | tf_op jit(solution)/shard_map/all_gather | solution.py:42
  24.1 2.4 stack.2
  26.5 4.7 all-to-all-start
  31.3 53.3 %all_gather.6 = bf16[1024,256]{0,1:T(8,128)(2,1)S(1)} all-gather(bf16[1024,32]{0,1:T(8,128)(2,1)S(1)} %copy-done), channel_id=1, replica_groups=mesh['rows'=8,'cols'=4] {'rows'}, dimensions={1}, use_global_device_ids=true | all-gather | bytes 589824 | tf_op jit(solution)/shard_map/all_gather | solution.py:41
  84.6 1.0 fusion.24
  86.7 6.4 %copy.34 = bf16[8192,256]{1,0:T(8,128)(2,1)} copy(bf16[8192,256]{0,1:T(8,128)(2,1)} %bitcast.1) | data formatting | bytes 8388608
  93.0 29.2 %all-reduce.3.cloned.1.call-done = f32[256,256]{0,1:T(8,128)} async-done(((f32[256,256]{0,1:T(8,128)}), f32[256,256]{0,1:T(8,128)}) %all-reduce.3.cloned.1.call-update) | async-done | bytes 262160 | tf_op jit(solution)/shard_map/psum | solution.py:48
  122.2 4.7 fusion.11
  127.2 11.7 %cholesky.50 = f32[128,128]{1,0:T(8,128)S(1)} custom-call(f32[128,128]{1,0:T(8,128)S(1)} %cholesky.118), custom_call_target="Cholesky" | custom-call | tf_op jit(solution)/shard_map/jit(cholesky)/cholesky | solution.py:79
  138.9 9.8 %custom-call.18 = f32[1,128,128]{1,2,0:T(8,128)S(1)} custom-call(f32[1,128,128]{2,1,0:T(8,128)S(1)} %get-tuple-element.300), custom_call_target="InvertDiagBlocksLowerTriangular" | custom-call | tf_op jit(solution)/shard_map/jit(cholesky)/cholesky | solution.py:79
  149.2 11.7 %cholesky.105 = f32[128,128]{1,0:T(8,128)S(1)} custom-call(f32[128,128]{1,0:T(8,128)S(1)} %convolution_subtract_fusion.2), custom_call_target="Cholesky" | custom-call | tf_op jit(solution)/shard_map/jit(cholesky)/cholesky | solution.py:79
  161.0 223.7 %while.15 = (s32[]{:T(128)}, f32[512,256]{1,0:T(8,128)S(1)}, s32[]{:T(128)}, s32[512]{0:T(512)}, s32[]{:T(128)}, /*index=5*/s32[512]{0:T(512)}, s32[]{:T(128)}, ...) while((s32[]{:T(128)}, f32[512,256]{1,0:T(8,128)S(1)}, ...), condition=%wide.region_7.8_spmd.clone, body=%wide.region_5.7_spmd.clone.sunk | while | flops 214271872 | bytes 27305452 | solution.py:77
  162.6 0.9 fusion.42
  163.5 0.9 constant_dynamic-slice_fusion.5
  164.4 63.5 %gather_fusion = bf16[16384,256]{1,0:T(8,128)(2,1)} fusion(bf16[8192,256]{1,0:T(8,128)(2,1)} %get-tuple-element.464, s32[16384]{0:T(1024)S(1)} %broadcast_clamp_fusion.2), kind=kCustom, calls=%fused_computation.1.clone.clone.1 | custom fusion | bytes 16842752 | tf_op jit(solution)/shard_map/while/body/gather | solution.py:17
  227.9 5.5 %fusion.43 = f32[128,256]{1,0:T(8,128)S(1)} fusion(f32[128,128]{1,0:T(8,128)S(1)} %fusion.42, bf16[16384,256]{1,0:T(8,128)(2,1)} %gather_fusion), kind=kLoop, calls=%fused_computation.7.clone.1 | loop fusion | flops 12550144 | bytes 8585216 | tf_op jit(solution)/shard_map/while/body/reduce_sum | solution.py:19
  237.1 0.9 fusion.42
  238.9 63.5 %gather_fusion = bf16[16384,256]{1,0:T(8,128)(2,1)} fusion(bf16[8192,256]{1,0:T(8,128)(2,1)} %get-tuple-element.464, s32[16384]{0:T(1024)S(1)} %broadcast_clamp_fusion.2), kind=kCustom, calls=%fused_computation.1.clone.clone.1 | custom fusion | bytes 16842752 | tf_op jit(solution)/shard_map/while/body/gather | solution.py:17
  302.4 5.5 %fusion.43 = f32[128,256]{1,0:T(8,128)S(1)} fusion(f32[128,128]{1,0:T(8,128)S(1)} %fusion.42, bf16[16384,256]{1,0:T(8,128)(2,1)} %gather_fusion), kind=kLoop, calls=%fused_computation.7.clone.1 | loop fusion | flops 12550144 | bytes 8585216 | tf_op jit(solution)/shard_map/while/body/reduce_sum | solution.py:19
  311.6 0.9 fusion.42
  313.4 63.5 %gather_fusion = bf16[16384,256]{1,0:T(8,128)(2,1)} fusion(bf16[8192,256]{1,0:T(8,128)(2,1)} %get-tuple-element.464, s32[16384]{0:T(1024)S(1)} %broadcast_clamp_fusion.2), kind=kCustom, calls=%fused_computation.1.clone.clone.1 | custom fusion | bytes 16842752 | tf_op jit(solution)/shard_map/while/body/gather | solution.py:17
  376.9 5.5 %fusion.43 = f32[128,256]{1,0:T(8,128)S(1)} fusion(f32[128,128]{1,0:T(8,128)S(1)} %fusion.42, bf16[16384,256]{1,0:T(8,128)(2,1)} %gather_fusion), kind=kLoop, calls=%fused_computation.7.clone.1 | loop fusion | flops 12550144 | bytes 8585216 | tf_op jit(solution)/shard_map/while/body/reduce_sum | solution.py:19
  384.7 1.0 copy.35
  387.8 3.9 while.14
  388.4 1.3 bitcast_dynamic-update-slice_fusion.2
  390.3 1.3 bitcast_dynamic-update-slice_fusion.2
  391.7 19.7 %custom-call.19 = f32[2,128,128]{1,2,0:T(8,128)S(1)} custom-call(f32[2,128,128]{2,1,0:T(8,128)S(1)} %get-tuple-element.189), custom_call_target="InvertDiagBlocksLowerTriangular" | custom-call | tf_op jit(solution)/shard_map/jit(_cho_solve)/triangular_solve | solution.py:80
  411.4 70.7 %reduce-scatter.2.cloned.1.call-done = f32[128,256]{0,1:T(8,128)} async-done(((f32[512,256]{0,1:T(8,128)}), f32[128,256]{0,1:T(8,128)}) %reduce-scatter.2.cloned.1.call-update) | async-done | bytes 131088 | tf_op jit(solution)/shard_map/reduce_scatter | solution.py:78
  482.1 1.1 fusion.13
  483.3 1.0 convolution_subtract_fusion.1
  485.3 11.8 %all_to_all.30 = f32[128,8,32]{0,2,1:T(8,128)S(1)} all-to-all(f32[128,8,32]{0,2,1:T(8,128)S(1)} %bitcast.70), channel_id=1, replica_groups=mesh['rows'=8,'cols'=4] {'rows'}, dimensions={1} | all-to-all | bytes 262144 | tf_op jit(solution)/shard_map/all_to_all | solution.py:82
  497.3 10.2 %all_to_all.31 = f32[4,256,32]{1,2,0:T(8,128)S(1)} all-to-all(f32[4,256,32]{1,2,0:T(8,128)S(1)} %copy.37), channel_id=1, replica_groups=mesh['rows'=8,'cols'=4] {'cols'}, dimensions={0} | all-to-all | bytes 262144 | tf_op jit(solution)/shard_map/all_to_all | solution.py:81
  (63 shorter events, 18.1 us)
Async XLA Ops:
  26.5 4.8 copy-start
  26.5 60.1 %all-to-all-start = ((bf16[8,8192,32]{1,2,0:T(8,128)(2,1)}), bf16[8,8192,32]{1,2,0:T(8,128)(2,1)}, u32[]{:S(2)}, u32[]{:S(2)}) async-start(bf16[8,8192,32]{1,2,0:T(8,128)(2,1)} %stack.2), calls=%async_computation | async-start | bytes 8388608 | tf_op jit(solution)/shard_map/all_to_all | solution.py:44
  31.2 91.0 %all-reduce.3.cloned.1.call-start = ((), (), s32[]{:S(2)}) async-start(), calls=%async_computation.4 | async-start | bytes 524288 | tf_op jit(solution)/shard_map/psum | solution.py:48
  85.7 396.4 %reduce-scatter.2.cloned.1.call-start = ((), (), s32[]{:S(2)}) async-start(), calls=%async_computation.5 | async-start | bytes 655360 | tf_op jit(solution)/shard_map/reduce_scatter | solution.py:78
Sparse Core Ops, SparseCore 0:
  85.8 36.3 all-reduce.2
  385.8 96.2 reduce-scatter.1
